TPU v7x, 32 devices: a whole 2x2x4 slice. The times are simulated.
32 devices in a mesh: ctx: 8 (over z, x), dp: 4 (over y, core).
Axes of the slice: x: 2, y: 2, z: 4, core: 2. Of those that a mesh axis runs over, the one named last changes fastest.
Arguments:
- queries: bfloat16 [4, 2048, 1024], P('dp', 'ctx'), may hold values from -8 to 8
- keys: bfloat16 [4, 2048, 1024], P('dp', 'ctx'), may hold values from -8 to 8
- values: bfloat16 [4, 2048, 1024], P('dp', 'ctx'), may hold values from -6 to 6
- cotangent: bfloat16 [4, 2048, 2048], P('dp', 'ctx'), may hold values from -6 to 6
- proj_weight: bfloat16 [1024, 2048], P('dp'), may hold values from -0.1875 to 0.1875
- pattern: int32 [4, 8, 16, 2], P('dp'), may hold values 0 or 1
Outputs:
- projected: bfloat16 [4, 2048, 2048], P('dp', 'ctx')
- grad_query: bfloat16 [4, 2048, 1024], P('dp', 'ctx')
- grad_key: bfloat16 [4, 2048, 1024], P('dp', 'ctx')
- grad_value: bfloat16 [4, 2048, 1024], P('dp', 'ctx')
- grad_proj: float32 [1024, 2048], P('dp', 'ctx')
Inputs may be any that keep to these rules, and one draw needn't show every extreme that they name: `pattern`: entries with o = 0 or with q - o < 1 are not read.
All inputs are finite; a program needn't handle non-finite values. No bound on the sum of `pattern` on one device may be relied on, other than what follows from the above.
Results may differ from a plain program's by a relative error of at most 0.0085.
The roundings to bfloat16 on the way count: a program that leaves them out, or rounds other values in their place, can miss the bound.
Values may be sent and summed in bfloat16 or wider, within the bound.
No kernel may reach another device: no remote copies, remote signals or barrier semaphores. Data moves between devices by JAX's collectives and lax.ppermute only.
A program may use at most 128 MiB of HBM per device.

v0:
```python
import jax
import jax.numpy as jnp
from jax import lax
from jax.sharding import PartitionSpec as P

HEADS = 8
HDIM = 128
BLK = 128
BLK_DEV = 2
WIN = 2
masked_value = -1e30


def shifted(value, axis, steps):
    count = lax.axis_size(axis)
    leading, last = (max(0, -steps), min(count, count - steps))
    return lax.ppermute(value, axis, [(source, source + steps) for source in range(leading, last)])


def spread(block, axis, holder):
    block = jnp.where(lax.axis_index(axis) == holder, block, jnp.zeros_like(block))
    return lax.psum(block, axis)


def product(form, left, right):
    return jnp.einsum(form, left, right, preferred_element_type=jnp.float32)


def block_masks(pattern_rows, query_blocks):
    column = jnp.arange(WIN * BLK, dtype=jnp.int32)
    within = jnp.arange(BLK, dtype=jnp.int32)
    offsets = WIN - 1 - jnp.arange(WIN, dtype=jnp.int32)
    flipped = jnp.flip(pattern_rows, axis=2) == 1
    key_blocks = query_blocks[:, None] - offsets[None, :]
    permitted = (flipped | (offsets == 0)[None, None, :]) & (key_blocks >= 1)[:, None, :]
    expanded = jnp.repeat(permitted, BLK, axis=2)
    causal = (column[None, :] < (WIN - 1) * BLK) | (
        column[None, :] - (WIN - 1) * BLK <= within[:, None]
    )
    key_mask = expanded[:, :, None, :] & causal[None, None, :, :]
    sink_mask = (query_blocks[:, None, None] > 0) | (within[None, None, :] <= within[None, :, None])
    return (key_mask, sink_mask[:, None, :, :])


def attend_scores(queries_b, key_window, sink_keys, key_mask, sink_mask):
    inverse_root = HDIM ** (-0.5)
    scores = product("nqhd,nkhd->nhqk", queries_b, key_window) * inverse_root
    sink_scores = product("nqhd,khd->nhqk", queries_b, sink_keys) * inverse_root
    return (
        jnp.where(key_mask, scores, masked_value),
        jnp.where(sink_mask, sink_scores, masked_value),
    )


def forward_blocks(
    queries_b, key_window, value_window, sink_keys, sink_values, key_mask, sink_mask
):
    scores, sink_scores = attend_scores(queries_b, key_window, sink_keys, key_mask, sink_mask)
    row_max = jnp.maximum(jnp.max(scores, axis=-1), jnp.max(sink_scores, axis=-1))
    row_total = jnp.sum(jnp.exp(scores - row_max[..., None]), axis=-1) + jnp.sum(
        jnp.exp(sink_scores - row_max[..., None]), axis=-1
    )
    log_total = row_max + jnp.log(row_total)
    weights = jnp.exp(scores - log_total[..., None]).astype(jnp.bfloat16)
    sink_weights = jnp.exp(sink_scores - log_total[..., None]).astype(jnp.bfloat16)
    attended = product("nhqk,nkhd->nqhd", weights, value_window) + product(
        "nhqk,khd->nqhd", sink_weights, sink_values
    )
    return (attended.astype(jnp.bfloat16), log_total)


def backward_blocks(
    queries_b,
    key_window,
    value_window,
    sink_keys,
    sink_values,
    key_mask,
    sink_mask,
    log_total,
    out_grad,
    row_delta,
):
    inverse_root = HDIM ** (-0.5)
    scores, sink_scores = attend_scores(queries_b, key_window, sink_keys, key_mask, sink_mask)
    weights = jnp.exp(scores - log_total[..., None])
    sink_weights = jnp.exp(sink_scores - log_total[..., None])
    prob_grad = product("nqhd,nkhd->nhqk", out_grad, value_window)
    sink_prob_grad = product("nqhd,khd->nhqk", out_grad, sink_values)
    score_grad = (weights * (prob_grad - row_delta[..., None])).astype(jnp.bfloat16)
    sink_score_grad = (sink_weights * (sink_prob_grad - row_delta[..., None])).astype(jnp.bfloat16)
    query_grad = inverse_root * (
        product("nhqk,nkhd->nqhd", score_grad, key_window)
        + product("nhqk,khd->nqhd", sink_score_grad, sink_keys)
    )
    window_key_grad = inverse_root * product("nhqk,nqhd->nkhd", score_grad, queries_b)
    window_value_grad = product("nhqk,nqhd->nkhd", weights.astype(jnp.bfloat16), out_grad)
    sink_key_grad = inverse_root * product("nhqk,nqhd->khd", sink_score_grad, queries_b)
    sink_value_grad = product("nhqk,nqhd->khd", sink_weights.astype(jnp.bfloat16), out_grad)
    return (query_grad, window_key_grad, window_value_grad, sink_key_grad, sink_value_grad)


def make_windows(extended, first):
    pieces = [
        extended[(number + first) * BLK : (number + first + WIN) * BLK] for number in range(BLK_DEV)
    ]
    return jnp.stack(pieces).reshape(BLK_DEV, WIN * BLK, HEADS, HDIM)


def place_windows(window_grad):
    flat = window_grad.reshape(BLK_DEV, WIN * BLK, HEADS * HDIM)
    placed = jnp.zeros((2 * BLK_DEV * BLK, HEADS * HDIM), jnp.float32)
    for number in range(BLK_DEV):
        placed = placed + jnp.pad(
            flat[number], (((number + 1) * BLK, (2 * BLK_DEV - number - 1 - WIN) * BLK), (0, 0))
        )
    return placed


def body(queries, keys, values, cotangent, proj_weight, pattern):
    query_rows = queries[0]
    key_rows = keys[0]
    value_rows = values[0]
    grad_output = cotangent[0]
    pattern_doc = pattern[0]
    rows = query_rows.shape[0]
    width_heads = query_rows.shape[1]
    context_index = lax.axis_index("ctx")
    context_count = lax.axis_size("ctx")
    document_count = lax.axis_size("dp")
    prev_keys, prev_values = shifted((key_rows, value_rows), "ctx", 1)
    first_keys, first_values = (
        spread(key_rows[:BLK], "ctx", 0),
        spread(value_rows[:BLK], "ctx", 0),
    )
    full_weight = lax.all_gather(proj_weight, "dp", axis=0, tiled=True)
    query_blocks = context_index * BLK_DEV + jnp.arange(BLK_DEV, dtype=jnp.int32)
    pattern_rows = jnp.transpose(
        lax.dynamic_slice_in_dim(pattern_doc, context_index * BLK_DEV, BLK_DEV, 1), (1, 0, 2)
    )
    key_mask, sink_mask = block_masks(pattern_rows, query_blocks)
    key_window = make_windows(jnp.concatenate([prev_keys, key_rows], axis=0), 1)
    value_window = make_windows(jnp.concatenate([prev_values, value_rows], axis=0), 1)
    query_blocked = query_rows.reshape(BLK_DEV, BLK, HEADS, HDIM)
    sink_keys = first_keys.reshape(BLK, HEADS, HDIM)
    sink_values = first_values.reshape(BLK, HEADS, HDIM)
    attended, log_total = forward_blocks(
        query_blocked, key_window, value_window, sink_keys, sink_values, key_mask, sink_mask
    )
    attended_rows = attended.reshape(rows, width_heads)
    projected = jnp.dot(attended_rows, full_weight, preferred_element_type=jnp.float32).astype(
        jnp.bfloat16
    )
    grad_attended = lax.dot_general(
        grad_output, full_weight, (((1,), (1,)), ((), ())), preferred_element_type=jnp.float32
    ).astype(jnp.bfloat16)
    weight_scale = float(rows * context_count * document_count) ** (-0.5)
    partial_sum = lax.psum_scatter(
        lax.dot_general(
            attended_rows, grad_output, (((0,), (0,)), ((), ())), preferred_element_type=jnp.float32
        )
        * weight_scale,
        "dp",
        scatter_dimension=0,
        tiled=True,
    )
    grad_proj = lax.psum_scatter(partial_sum, "ctx", scatter_dimension=1, tiled=True)
    row_delta = jnp.sum(
        grad_attended.astype(jnp.float32).reshape(rows, HEADS, HDIM)
        * attended_rows.astype(jnp.float32).reshape(rows, HEADS, HDIM),
        axis=-1,
    )
    delta_blocked = jnp.transpose(row_delta.reshape(BLK_DEV, BLK, HEADS), (0, 2, 1))
    grad_blocked = grad_attended.reshape(BLK_DEV, BLK, HEADS, HDIM)
    query_grad, window_key, window_value, sink_key, sink_value = backward_blocks(
        query_blocked,
        key_window,
        value_window,
        sink_keys,
        sink_values,
        key_mask,
        sink_mask,
        log_total,
        grad_blocked,
        delta_blocked,
    )
    sink_key_sum, sink_value_sum = lax.psum((sink_key, sink_value), "ctx")
    placed_keys = place_windows(window_key)
    placed_values = place_windows(window_value)
    later_keys, later_values = shifted((placed_keys[:rows], placed_values[:rows]), "ctx", -1)
    own_key = placed_keys[rows:] + later_keys
    own_value = placed_values[rows:] + later_values
    leading = (context_index == 0).astype(jnp.float32)
    own_key = jnp.concatenate(
        [own_key[:BLK] + leading * sink_key_sum.reshape(BLK, width_heads), own_key[BLK:]], axis=0
    )
    own_value = jnp.concatenate(
        [own_value[:BLK] + leading * sink_value_sum.reshape(BLK, width_heads), own_value[BLK:]],
        axis=0,
    )
    return (
        projected[None],
        query_grad.reshape(rows, width_heads).astype(jnp.bfloat16)[None],
        own_key.astype(jnp.bfloat16)[None],
        own_value.astype(jnp.bfloat16)[None],
        grad_proj,
    )


def solution(mesh):
    return jax.shard_map(
        body,
        mesh=mesh,
        in_specs=(
            P("dp", "ctx", None),
            P("dp", "ctx", None),
            P("dp", "ctx", None),
            P("dp", "ctx", None),
            P("dp", None),
            P("dp", None, None, None),
        ),
        out_specs=(
            P("dp", "ctx", None),
            P("dp", "ctx", None),
            P("dp", "ctx", None),
            P("dp", "ctx", None),
            P("dp", "ctx"),
        ),
        check_vma=False,
    )
```

profile of v0, /device:TPU:0, one launch (start us, length us, event | category | flops | bytes accessed | tf_op | source)
XLA Modules:
  0.0 304.7 jit_solution(7784377283178281256)
XLA Ops:
  13.1 5.7 %collective-permute-start = (bf16[256,1024]{0,1:T(8,128)(2,1)S(1)}, bf16[256,1024]{0,1:T(8,128)(2,1)}, u32[]{:S(2)}, u32[]{:S(2)}) collective-permute-start(bf16[256,1024]{0,1:T(8,128)(2,1)S(1)} %bitcast.149), channel_id=1, source_target_pairs={{0,4},{4,8},{8,12},{12,16},{16,20},{20,24},{24,28},{1,5},{5,9},{9,... | collective-permute-start | bytes 1572872 | tf_op jit(solution)/shard_map/ppermute | solution.py:17
  18.8 3.4 %collective-permute-start.1 = (bf16[256,1024]{0,1:T(8,128)(2,1)S(1)}, bf16[256,1024]{0,1:T(8,128)(2,1)}, u32[]{:S(2)}, u32[]{:S(2)}) collective-permute-start(bf16[256,1024]{0,1:T(8,128)(2,1)S(1)} %bitcast.146), channel_id=1, source_target_pairs={{0,4},{4,8},{8,12},{12,16},{16,20},{20,24},{24,28},{1,5},{5,9},{9,... | collective-permute-start | bytes 1572872 | tf_op jit(solution)/shard_map/ppermute | solution.py:17
  26.2 5.9 %collective-permute-done = bf16[256,1024]{0,1:T(8,128)(2,1)} collective-permute-done((bf16[256,1024]{0,1:T(8,128)(2,1)S(1)}, bf16[256,1024]{0,1:T(8,128)(2,1)}, u32[]{:S(2)}, u32[]{:S(2)}) %collective-permute-start) | collective-permute-done | bytes 524320 | tf_op jit(solution)/shard_map/ppermute | solution.py:17
  34.1 9.0 %collective-permute-done.1 = bf16[256,1024]{0,1:T(8,128)(2,1)} collective-permute-done((bf16[256,1024]{0,1:T(8,128)(2,1)S(1)}, bf16[256,1024]{0,1:T(8,128)(2,1)}, u32[]{:S(2)}, u32[]{:S(2)}) %collective-permute-start.1) | collective-permute-done | bytes 524320 | tf_op jit(solution)/shard_map/ppermute | solution.py:17
  45.1 49.3 %all-reduce.11.cloned.1.call-done = (bf16[128,8,128]{2,0,1:T(8,128)(2,1)}, bf16[128,8,128]{2,0,1:T(8,128)(2,1)}) async-done(((bf16[128,8,128]{2,0,1:T(8,128)(2,1)}, bf16[128,8,128]{2,0,1:T(8,128)(2,1)}), (bf16[128,8,128]{2,0,1:T(8,128)(2,1)}, bf16[128,8,128]{2,0,1:T(8,128)(2,1)})) %all-reduce.11.cloned.1.call-update) | async-done | bytes 524304 | tf_op jit(solution)/shard_map/psum | solution.py:22
  95.7 2.4 fusion.48
  102.5 4.6 %convolution_multiply_fusion = f32[1024,2048]{1,0:T(8,128)} fusion(bf16[1,256,2048]{2,1,0:T(8,128)(2,1)S(1)} %copy-done, bf16[32,8,8,128]{3,2,1,0:T(8,128)(2,1)S(1)} %bitcast.156), kind=kOutput, calls=%fused_computation | convolution fusion | flops 1075838976 | bytes 9961472 | tf_op jit(solution)/shard_map/dot_general | solution.py:159
  107.2 2.3 copy.155
  109.5 3.5 %convolution_convert_fusion.1 = bf16[256,1024]{1,0:T(8,128)(2,1)S(1)} fusion(bf16[1024,2048]{1,0:T(8,128)(2,1)} %all-gather.2.cloned.1.call-done, bf16[1,256,2048]{2,1,0:T(8,128)(2,1)S(1)} %copy-done), kind=kOutput, calls=%fused_computation.30 | convolution fusion | flops 1074003968 | bytes 5767168 | tf_op jit(solution)/shard_map/dot_general | solution.py:154
  116.4 2.2 copy.174
  119.5 2.8 convolution_bitcast_fusion.6
  124.8 2.1 copy.172
  132.1 2.1 copy.164
  134.2 2.1 convert_element_type.79
  136.3 41.4 %reduce-scatter.3.cloned.1.call-done = f32[256,2048]{1,0:T(8,128)} async-done(((f32[1024,2048]{1,0:T(8,128)}), f32[256,2048]{1,0:T(8,128)}) %reduce-scatter.3.cloned.1.call-update) | async-done | bytes 2097168 | tf_op jit(solution)/shard_map/reduce_scatter | solution.py:158
  181.0 2.5 copy.169
  183.5 2.5 copy.168
  186.0 2.3 pad_add_fusion.1
  193.5 2.2 fusion
  195.8 9.9 %all-reduce.9.cloned.1.call-done = (f32[128,8,128]{2,0,1:T(8,128)}, f32[128,8,128]{2,0,1:T(8,128)}) async-done(((f32[128,8,128]{2,0,1:T(8,128)}, f32[128,8,128]{2,0,1:T(8,128)}), (f32[128,8,128]{2,0,1:T(8,128)}, f32[128,8,128]{2,0,1:T(8,128)})) %all-reduce.9.cloned.1.call-update) | async-done | bytes 1048592 | tf_op jit(solution)/shard_map/psum | solution.py:187
  209.6 7.0 %collective-permute-done.2 = f32[256,1024]{0,1:T(8,128)} collective-permute-done((f32[256,1024]{0,1:T(8,128)}, f32[256,1024]{0,1:T(8,128)}, u32[]{:S(2)}, u32[]{:S(2)}) %collective-permute-start.2) | collective-permute-done | bytes 1048608 | tf_op jit(solution)/shard_map/ppermute | solution.py:17
  218.9 2.1 copy.178
  224.9 18.4 %collective-permute-done.3 = f32[256,1024]{0,1:T(8,128)} collective-permute-done((f32[256,1024]{0,1:T(8,128)}, f32[256,1024]{0,1:T(8,128)}, u32[]{:S(2)}, u32[]{:S(2)}) %collective-permute-start.3) | collective-permute-done | bytes 1048608 | tf_op jit(solution)/shard_map/ppermute | solution.py:17
  245.9 51.6 %reduce-scatter.5.cloned.1.call-done = f32[256,256]{1,0:T(8,128)} async-done(((f32[256,2048]{1,0:T(8,128)}), f32[256,256]{1,0:T(8,128)}) %reduce-scatter.5.cloned.1.call-update) | async-done | bytes 262160 | tf_op jit(solution)/shard_map/reduce_scatter | solution.py:167
  (144 shorter events, 51.7 us)
Async XLA Ops:
  8.0 94.5 %copy-start = (bf16[1,256,2048]{2,1,0:T(8,128)(2,1)S(1)}, bf16[1,256,2048]{2,1,0:T(8,128)(2,1)}, u32[]{:S(2)}) copy-start(bf16[1,256,2048]{2,1,0:T(8,128)(2,1)} %param.9) | copy-start | bytes 3145732
  8.0 86.4 %all-reduce.11.cloned.1.call-start = ((), (), s32[]{:S(2)}) async-start(), calls=%async_computation.6 | async-start | bytes 1048576 | tf_op jit(solution)/shard_map/psum | solution.py:22
  10.7 12.5 %copy-start.28 = (bf16[1,256,1024]{2,1,0:T(8,128)(2,1)S(1)}, bf16[1,256,1024]{2,1,0:T(8,128)(2,1)}, u32[]{:S(2)}) copy-start(bf16[1,256,1024]{2,1,0:T(8,128)(2,1)} %param.6) | copy-start | bytes 1572868
  12.5 97.0 %all-gather.2.cloned.1.call-start = ((), (), s32[]{:S(2)}) async-start(), calls=%async_computation.2 | async-start | bytes 5242880 | tf_op jit(solution)/shard_map/all_gather | solution.py:136
  13.0 164.7 %reduce-scatter.3.cloned.1.call-start = ((), (), s32[]{:S(2)}) async-start(), calls=%async_computation.3 | async-start | bytes 10485760 | tf_op jit(solution)/shard_map/reduce_scatter | solution.py:158
  13.1 19.0 %collective-permute-start = (bf16[256,1024]{0,1:T(8,128)(2,1)S(1)}, bf16[256,1024]{0,1:T(8,128)(2,1)}, u32[]{:S(2)}, u32[]{:S(2)}) collective-permute-start(bf16[256,1024]{0,1:T(8,128)(2,1)S(1)} %bitcast.149), channel_id=1, source_target_pairs={{0,4},{4,8},{8,12},{12,16},{16,20},{20,24},{24,28},{1,5},{5,9},{9,... | collective-permute-start | bytes 1572872 | tf_op jit(solution)/shard_map/ppermute | solution.py:17
  18.8 24.3 %collective-permute-start.1 = (bf16[256,1024]{0,1:T(8,128)(2,1)S(1)}, bf16[256,1024]{0,1:T(8,128)(2,1)}, u32[]{:S(2)}, u32[]{:S(2)}) collective-permute-start(bf16[256,1024]{0,1:T(8,128)(2,1)S(1)} %bitcast.146), channel_id=1, source_target_pairs={{0,4},{4,8},{8,12},{12,16},{16,20},{20,24},{24,28},{1,5},{5,9},{9,... | collective-permute-start | bytes 1572872 | tf_op jit(solution)/shard_map/ppermute | solution.py:17
  23.3 71.1 %copy-start.10 = (bf16[32,8,8,128]{3,2,1,0:T(8,128)(2,1)}, bf16[32,8,8,128]{3,2,1,0:T(8,128)(2,1)S(1)}, u32[]{:S(2)}) copy-start(bf16[32,8,8,128]{3,2,1,0:T(8,128)(2,1)S(1)} %copy.199) | copy-start | bytes 1572868
  95.7 4.2 %copy-start.1 = (f32[2,8,128,128]{2,3,0,1:T(8,128)}, f32[2,8,128,128]{2,3,0,1:T(8,128)S(1)}, u32[]{:S(2)}) copy-start(f32[2,8,128,128]{2,3,0,1:T(8,128)S(1)} %get-tuple-element.31) | copy-start | bytes 3145732
  107.1 98.5 %all-reduce.9.cloned.1.call-start = ((), (), s32[]{:S(2)}) async-start(), calls=%async_computation.5 | async-start | bytes 2097152 | tf_op jit(solution)/shard_map/psum | solution.py:187
  118.6 3.6 %copy-start.2 = (f32[2,8,128,128]{2,3,0,1:T(8,128)S(1)}, f32[2,8,128,128]{2,3,0,1:T(8,128)}, u32[]{:S(2)}) copy-start(f32[2,8,128,128]{2,3,0,1:T(8,128)} %copy-done.1) | copy-start | bytes 3145732
  118.6 3.6 %copy-start.18 = (bf16[2,128,8,128]{1,3,0,2:T(8,128)(2,1)S(1)}, bf16[2,128,8,128]{1,3,0,2:T(8,128)(2,1)}, u32[]{:S(2)}) copy-start(bf16[2,128,8,128]{1,3,0,2:T(8,128)(2,1)} %copy.174) | copy-start | bytes 1572868
  119.5 3.9 %copy-start.11 = (bf16[32,8,8,128]{3,2,1,0:T(8,128)(2,1)S(1)}, bf16[32,8,8,128]{3,2,1,0:T(8,128)(2,1)}, u32[]{:S(2)}) copy-start(bf16[32,8,8,128]{3,2,1,0:T(8,128)(2,1)} %copy-done.10) | copy-start | bytes 1572868
  123.4 3.5 %copy-start.29 = (f32[256,8]{0,1:T(8,128)S(1)}, f32[256,8]{0,1:T(8,128)}, u32[]{:S(2)}) copy-start(f32[256,8]{0,1:T(8,128)} %copy.156) | copy-start | bytes 24580
  124.5 173.0 %reduce-scatter.5.cloned.1.call-start = ((), (), s32[]{:S(2)}) async-start(), calls=%async_computation.4 | async-start | bytes 2359296 | tf_op jit(solution)/shard_map/reduce_scatter | solution.py:167
  186.0 3.6 %copy-start.12 = (bf16[2,128,8,128]{1,3,2,0:T(8,128)(2,1)S(1)}, bf16[2,128,8,128]{1,3,2,0:T(8,128)(2,1)}, u32[]{:S(2)}) copy-start(bf16[2,128,8,128]{1,3,2,0:T(8,128)(2,1)} %copy.172) | copy-start | bytes 1572868
  188.3 28.2 %collective-permute-start.2 = (f32[256,1024]{0,1:T(8,128)}, f32[256,1024]{0,1:T(8,128)}, u32[]{:S(2)}, u32[]{:S(2)}) collective-permute-start(f32[256,1024]{0,1:T(8,128)} %pad_add_fusion.1), channel_id=1, source_target_pairs={{4,0},{8,4},{12,8},{16,12},{20,16},{24,20},{28,24},{5,1},{9,5},{13... | collective-permute-start | bytes 3145736 | tf_op jit(solution)/shard_map/ppermute | solution.py:17
  191.3 52.0 %collective-permute-start.3 = (f32[256,1024]{0,1:T(8,128)}, f32[256,1024]{0,1:T(8,128)}, u32[]{:S(2)}, u32[]{:S(2)}) collective-permute-start(f32[256,1024]{0,1:T(8,128)} %pad_add_fusion), channel_id=1, source_target_pairs={{4,0},{8,4},{12,8},{16,12},{20,16},{24,20},{28,24},{5,1},{9,5},{13... | collective-permute-start | bytes 3145736 | tf_op jit(solution)/shard_map/ppermute | solution.py:17
  195.8 20.8 %copy-start.4 = (f32[1,256,8,128]{1,3,2,0:T(8,128)S(1)}, f32[1,256,8,128]{1,3,2,0:T(8,128)}, u32[]{:S(2)}) copy-start(f32[1,256,8,128]{1,3,2,0:T(8,128)} %copy.169) | copy-start | bytes 3145732
  195.8 20.8 %copy-start.5 = (f32[1,256,8,128]{1,3,2,0:T(8,128)S(1)}, f32[1,256,8,128]{1,3,2,0:T(8,128)}, u32[]{:S(2)}) copy-start(f32[1,256,8,128]{1,3,2,0:T(8,128)} %copy.168) | copy-start | bytes 3145732
  209.6 8.4 %copy-start.22 = (f32[128,8,128]{0,2,1:T(8,128)S(1)}, f32[128,8,128]{0,2,1:T(8,128)}, u32[]{:S(2)}) copy-start(f32[128,8,128]{0,2,1:T(8,128)} %copy.171) | copy-start | bytes 1572868
  218.0 25.3 %copy-start.7 = (f32[1,256,8,128]{1,3,2,0:T(8,128)S(1)}, f32[1,256,8,128]{1,3,2,0:T(8,128)}, u32[]{:S(2)}) copy-start(f32[1,256,8,128]{1,3,2,0:T(8,128)} %copy-done.6) | copy-start | bytes 3145732
  218.0 25.3 %copy-start.9 = (f32[1,256,8,128]{1,3,2,0:T(8,128)S(1)}, f32[1,256,8,128]{1,3,2,0:T(8,128)}, u32[]{:S(2)}) copy-start(f32[1,256,8,128]{1,3,2,0:T(8,128)} %copy-done.8) | copy-start | bytes 3145732
  224.9 19.8 %copy-start.23 = (f32[128,8,128]{0,2,1:T(8,128)S(1)}, f32[128,8,128]{0,2,1:T(8,128)}, u32[]{:S(2)}) copy-start(f32[128,8,128]{0,2,1:T(8,128)} %copy.177) | copy-start | bytes 1572868
  (17 other events, 31.2 us)
Sparse Core Ops, SparseCore 0:
  12.9 81.4 all-reduce.10
  124.6 80.9 all-reduce.8
  209.8 87.7 reduce-scatter.4
Sparse Core Ops, SparseCore 1:
  14.5 37.0 all-gather.1
  107.2 70.4 reduce-scatter.2
where the time goes:
time: 306 us; the launch traced here: 305 us
  waiting for transfers between devices  193 us (63%)
  local copies, waits for them, and re-layouts  44.3 us (14%)
  matrix products  25 us (8%)
  between operations  15.7 us (5%)
  other arithmetic  14.2 us (5%)
  starting transfers between devices  12.3 us (4%)
    reduce_scatter x1, waiting for transfers between devices, body(): lax.psum_scatter(partial_sum, 'ctx', scatter_dimension=1, tiled=True)  51.6 us
    psum x1, waiting for transfers between devices, spread(): return lax.psum(block, axis)  49.3 us
    reduce_scatter x1, waiting for transfers between devices, body(): lax.psum_scatter(lax.dot_general(attended_rows, grad_output, (((0,), (0,)...  41.4 us
    ppermute x4, waiting for transfers between devices, shifted(): lax.ppermute(value, axis, [(source, source + steps) for source in range(l...  40.3 us
    dot_general x12, matrix products, product(): return jnp.einsum(form, left, right, preferred_element_type=jnp.float32)  14.7 us
    unnamed x71, local copies, waits for them, and re-layouts  13.7 us
    ppermute x4, starting transfers between devices, shifted(): lax.ppermute(value, axis, [(source, source + steps) for source in range(l...  11.9 us
    psum x1, waiting for transfers between devices, body(): sink_key_sum, sink_value_sum = lax.psum((sink_key, sink_value), 'ctx')  9.86 us
  transfers between devices with their start and end apart: 9, of which 8 were waited for; matrix products, arithmetic and copies ran while one was open for 24% of the time, Pallas kernels for 0%

commit v1 on v0

--- a/solution.py
+++ b/solution.py
@@ -19,7 +19,7 @@
 
 def spread(block, axis, holder):
     block = jnp.where(lax.axis_index(axis) == holder, block, jnp.zeros_like(block))
-    return lax.psum(block, axis)
+    return jnp.sum(lax.all_gather(block, axis), axis=0)
 
 
 def product(form, left, right):

time: 306 us -> 405 us (1.32)
  waiting for transfers between devices: 193 us -> 292 us
  other arithmetic: 14.2 us -> 22.2 us
  local copies, waits for them, and re-layouts: 44.3 us -> 37.4 us
    psum x1, waiting for transfers between devices: 9.86 us -> 79.1 us  [body(): sink_key_sum, sink_value_sum = lax.psum((sink_key, sink_value), 'ctx')]
    all_gather x0 -> x2, waiting for transfers between devices: none -> 69 us  [spread(): return jnp.sum(lax.all_gather(block, axis), axis=0)]
    psum x1 -> x0, waiting for transfers between devices: 49.3 us -> none  [spread(): return lax.psum(block, axis)]
    ppermute x4, waiting for transfers between devices: 40.3 us -> 13.7 us  [shifted(): lax.ppermute(value, axis, [(source, source + steps) for source in range(l...]
    all_gather x1, waiting for transfers between devices: 0.01 us -> 18.2 us  [body(): full_weight = lax.all_gather(proj_weight, 'dp', axis=0, tiled=True)]
    reduce_scatter x1, waiting for transfers between devices: 51.6 us -> 61.3 us  [body(): lax.psum_scatter(partial_sum, 'ctx', scatter_dimension=1, tiled=True)]
    reduce_scatter x1, waiting for transfers between devices: 41.4 us -> 49.6 us  [body(): lax.psum_scatter(lax.dot_general(attended_rows, grad_output, (((0,), (0,)...]
    reduce_sum x0 -> x2, other arithmetic: none -> 4.69 us  [spread(): return jnp.sum(lax.all_gather(block, axis), axis=0)]
  transfers between devices with their start and end apart: 9 -> 10, of which waited for: 8 -> 8; matrix products, arithmetic and copies ran while one was open for 24% -> 19% of each run, Pallas kernels for 0% -> 0%
where the time goes in v1:
time: 405 us; the launch traced here: 403 us
  waiting for transfers between devices  292 us (72%)
  local copies, waits for them, and re-layouts  37.4 us (9%)
  matrix products  25 us (6%)
  other arithmetic  22.2 us (5%)
  between operations  14.7 us (4%)
  starting transfers between devices  12.4 us (3%)
    psum x1, waiting for transfers between devices, body(): sink_key_sum, sink_value_sum = lax.psum((sink_key, sink_value), 'ctx')  79.1 us
    all_gather x2, waiting for transfers between devices, spread(): return jnp.sum(lax.all_gather(block, axis), axis=0)  69 us
    reduce_scatter x1, waiting for transfers between devices, body(): lax.psum_scatter(partial_sum, 'ctx', scatter_dimension=1, tiled=True)  61.3 us
    reduce_scatter x1, waiting for transfers between devices, body(): lax.psum_scatter(lax.dot_general(attended_rows, grad_output, (((0,), (0,)...  49.6 us
    all_gather x1, waiting for transfers between devices, body(): full_weight = lax.all_gather(proj_weight, 'dp', axis=0, tiled=True)  18.2 us
    dot_general x12, matrix products, product(): return jnp.einsum(form, left, right, preferred_element_type=jnp.float32)  14.8 us
    ppermute x4, waiting for transfers between devices, shifted(): lax.ppermute(value, axis, [(source, source + steps) for source in range(l...  13.7 us
    ppermute x4, starting transfers between devices, shifted(): lax.ppermute(value, axis, [(source, source + steps) for source in range(l...  12 us
  transfers between devices with their start and end apart: 10, of which 8 were waited for; matrix products, arithmetic and copies ran while one was open for 19% of the time, Pallas kernels for 0%

profile of v1, /device:TPU:0, one launch (start us, length us, event | category | flops | bytes accessed | tf_op | source)
XLA Modules:
  0.0 403.5 jit_solution(18224590047643842010)
XLA Ops:
  11.9 5.7 %collective-permute-start = (bf16[256,1024]{0,1:T(8,128)(2,1)S(1)}, bf16[256,1024]{0,1:T(8,128)(2,1)}, u32[]{:S(2)}, u32[]{:S(2)}) collective-permute-start(bf16[256,1024]{0,1:T(8,128)(2,1)S(1)} %bitcast.145), channel_id=1, source_target_pairs={{0,4},{4,8},{8,12},{12,16},{16,20},{20,24},{24,28},{1,5},{5,9},{9,... | collective-permute-start | bytes 1572872 | tf_op jit(solution)/shard_map/ppermute | solution.py:17
  17.8 3.5 collective-permute-start.1
  26.3 5.6 %collective-permute-done = bf16[256,1024]{0,1:T(8,128)(2,1)} collective-permute-done((bf16[256,1024]{0,1:T(8,128)(2,1)S(1)}, bf16[256,1024]{0,1:T(8,128)(2,1)}, u32[]{:S(2)}, u32[]{:S(2)}) %collective-permute-start) | collective-permute-done | bytes 524320 | tf_op jit(solution)/shard_map/ppermute | solution.py:17
  33.9 8.1 %collective-permute-done.1 = bf16[256,1024]{0,1:T(8,128)(2,1)} collective-permute-done((bf16[256,1024]{0,1:T(8,128)(2,1)S(1)}, bf16[256,1024]{0,1:T(8,128)(2,1)}, u32[]{:S(2)}, u32[]{:S(2)}) %collective-permute-start.1) | collective-permute-done | bytes 524320 | tf_op jit(solution)/shard_map/ppermute | solution.py:17
  45.9 23.6 %all-gather.4.cloned.1.call-done = bf16[8,128,1024]{2,1,0:T(8,128)(2,1)} async-done(((bf16[1,128,1024]{2,1,0:T(8,128)(2,1)}), bf16[8,128,1024]{2,1,0:T(8,128)(2,1)}) %all-gather.4.cloned.1.call-update) | async-done | bytes 2097168 | tf_op jit(solution)/shard_map/all_gather | solution.py:22
  72.3 2.3 fusion.47
  74.7 45.4 %all-gather.6.cloned.1.call-done = bf16[8,128,1024]{2,1,0:T(8,128)(2,1)} async-done(((bf16[1,128,1024]{2,1,0:T(8,128)(2,1)}), bf16[8,128,1024]{2,1,0:T(8,128)(2,1)}) %all-gather.6.cloned.1.call-update) | async-done | bytes 2097168 | tf_op jit(solution)/shard_map/all_gather | solution.py:22
  120.1 2.7 reduce_sum.54
  129.4 4.6 %convolution_multiply_fusion = f32[1024,2048]{1,0:T(8,128)} fusion(bf16[1,256,2048]{2,1,0:T(8,128)(2,1)S(1)} %copy-done, bf16[32,8,8,128]{3,2,1,0:T(8,128)(2,1)S(1)} %bitcast.154), kind=kOutput, calls=%fused_computation | convolution fusion | flops 1075838976 | bytes 9961472 | tf_op jit(solution)/shard_map/dot_general | solution.py:159
  134.1 2.4 copy.152
  136.5 18.2 %all-gather.8.cloned.1.call-done = bf16[1024,2048]{1,0:T(8,128)(2,1)} async-done(((bf16[256,2048]{1,0:T(8,128)(2,1)}), bf16[1024,2048]{1,0:T(8,128)(2,1)}) %all-gather.8.cloned.1.call-update) | async-done | bytes 4194320 | tf_op jit(solution)/shard_map/all_gather | solution.py:136
  154.7 3.5 convolution_convert_fusion.1
  161.3 2.1 copy.172
  164.2 2.4 convolution_bitcast_fusion.6
  170.5 2.1 multiply_convert_fusion
  174.8 2.1 copy.162
  176.9 2.1 convert_element_type.83
  178.9 49.6 %reduce-scatter.3.cloned.1.call-done = f32[256,2048]{1,0:T(8,128)} async-done(((f32[1024,2048]{1,0:T(8,128)}), f32[256,2048]{1,0:T(8,128)}) %reduce-scatter.3.cloned.1.call-update) | async-done | bytes 2097168 | tf_op jit(solution)/shard_map/reduce_scatter | solution.py:158
  233.1 2.6 copy.166
  235.6 2.2 pad_add_fusion.1
  242.6 2.2 fusion
  244.9 79.1 %all-reduce.7.cloned.1.call-done = (f32[128,8,128]{2,0,1:T(8,128)}, f32[128,8,128]{2,0,1:T(8,128)}) async-done(((f32[128,8,128]{2,0,1:T(8,128)}, f32[128,8,128]{2,0,1:T(8,128)}), (f32[128,8,128]{2,0,1:T(8,128)}, f32[128,8,128]{2,0,1:T(8,128)})) %all-reduce.7.cloned.1.call-update) | async-done | bytes 1048592 | tf_op jit(solution)/shard_map/psum | solution.py:187
  325.9 2.0 copy.169
  335.3 61.3 %reduce-scatter.5.cloned.1.call-done = f32[256,256]{1,0:T(8,128)} async-done(((f32[256,2048]{1,0:T(8,128)}), f32[256,256]{1,0:T(8,128)}) %reduce-scatter.5.cloned.1.call-update) | async-done | bytes 262160 | tf_op jit(solution)/shard_map/reduce_scatter | solution.py:167
  (149 shorter events, 53.4 us)
Async XLA Ops:
  7.2 122.3 %copy-start = (bf16[1,256,2048]{2,1,0:T(8,128)(2,1)S(1)}, bf16[1,256,2048]{2,1,0:T(8,128)(2,1)}, u32[]{:S(2)}) copy-start(bf16[1,256,2048]{2,1,0:T(8,128)(2,1)} %param.9) | copy-start | bytes 3145732
  7.2 10.4 %copy-start.25 = (bf16[1,256,1024]{2,1,0:T(8,128)(2,1)S(1)}, bf16[1,256,1024]{2,1,0:T(8,128)(2,1)}, u32[]{:S(2)}) copy-start(bf16[1,256,1024]{2,1,0:T(8,128)(2,1)} %param.7) | copy-start | bytes 1572868
  7.2 4.5 %copy-start.24 = (bf16[1,256,1024]{2,1,0:T(8,128)(2,1)S(1)}, bf16[1,256,1024]{2,1,0:T(8,128)(2,1)}, u32[]{:S(2)}) copy-start(bf16[1,256,1024]{2,1,0:T(8,128)(2,1)} %param.8) | copy-start | bytes 1572868
  7.2 62.4 %all-gather.4.cloned.1.call-start = ((), (), s32[]{:S(2)}) async-start(), calls=%async_computation.2 | async-start | bytes 2359296 | tf_op jit(solution)/shard_map/all_gather | solution.py:22
  9.1 111.0 %all-gather.6.cloned.1.call-start = ((), (), s32[]{:S(2)}) async-start(), calls=%async_computation.3 | async-start | bytes 2359296 | tf_op jit(solution)/shard_map/all_gather | solution.py:22
  10.9 143.8 %all-gather.8.cloned.1.call-start = ((), (), s32[]{:S(2)}) async-start(), calls=%async_computation.4 | async-start | bytes 5242880 | tf_op jit(solution)/shard_map/all_gather | solution.py:136
  11.6 216.9 %reduce-scatter.3.cloned.1.call-start = ((), (), s32[]{:S(2)}) async-start(), calls=%async_computation.5 | async-start | bytes 10485760 | tf_op jit(solution)/shard_map/reduce_scatter | solution.py:158
  11.9 20.0 %collective-permute-start = (bf16[256,1024]{0,1:T(8,128)(2,1)S(1)}, bf16[256,1024]{0,1:T(8,128)(2,1)}, u32[]{:S(2)}, u32[]{:S(2)}) collective-permute-start(bf16[256,1024]{0,1:T(8,128)(2,1)S(1)} %bitcast.145), channel_id=1, source_target_pairs={{0,4},{4,8},{8,12},{12,16},{16,20},{20,24},{24,28},{1,5},{5,9},{9,... | collective-permute-start | bytes 1572872 | tf_op jit(solution)/shard_map/ppermute | solution.py:17
  17.8 24.2 %collective-permute-start.1 = (bf16[256,1024]{0,1:T(8,128)(2,1)S(1)}, bf16[256,1024]{0,1:T(8,128)(2,1)}, u32[]{:S(2)}, u32[]{:S(2)}) collective-permute-start(bf16[256,1024]{0,1:T(8,128)(2,1)S(1)} %bitcast.142), channel_id=1, source_target_pairs={{0,4},{4,8},{8,12},{12,16},{16,20},{20,24},{24,28},{1,5},{5,9},{9,... | collective-permute-start | bytes 1572872 | tf_op jit(solution)/shard_map/ppermute | solution.py:17
  21.3 4.3 %copy-start.29 = (s32[1,8,16,2]{2,3,1,0:T(2,128)S(1)}, s32[1,8,16,2]{2,3,1,0:T(2,128)}, u32[]{:S(2)}) copy-start(s32[1,8,16,2]{2,3,1,0:T(2,128)} %param.11) | copy-start | bytes 3076
  23.4 10.4 %copy-start.8 = (bf16[32,8,8,128]{3,2,1,0:T(8,128)(2,1)}, bf16[32,8,8,128]{3,2,1,0:T(8,128)(2,1)S(1)}, u32[]{:S(2)}) copy-start(bf16[32,8,8,128]{3,2,1,0:T(8,128)(2,1)S(1)} %copy.201) | copy-start | bytes 1572868
  134.0 190.0 %all-reduce.7.cloned.1.call-start = ((), (), s32[]{:S(2)}) async-start(), calls=%async_computation.7 | async-start | bytes 2097152 | tf_op jit(solution)/shard_map/psum | solution.py:187
  159.3 4.8 %copy-start.3 = (f32[2,8,128,128]{2,3,0,1:T(8,128)S(1)}, f32[2,8,128,128]{2,3,0,1:T(8,128)}, u32[]{:S(2)}) copy-start(f32[2,8,128,128]{2,3,0,1:T(8,128)} %get-tuple-element.29) | copy-start | bytes 3145732
  163.4 3.1 copy-start.16
  164.2 3.5 copy-start.9
  168.8 227.8 %reduce-scatter.5.cloned.1.call-start = ((), (), s32[]{:S(2)}) async-start(), calls=%async_computation.6 | async-start | bytes 2359296 | tf_op jit(solution)/shard_map/reduce_scatter | solution.py:167
  235.6 3.5 copy-start.7
  237.8 90.1 %collective-permute-start.2 = (f32[256,1024]{0,1:T(8,128)}, f32[256,1024]{0,1:T(8,128)}, u32[]{:S(2)}, u32[]{:S(2)}) collective-permute-start(f32[256,1024]{0,1:T(8,128)} %pad_add_fusion.1), channel_id=1, source_target_pairs={{4,0},{8,4},{12,8},{16,12},{20,16},{24,20},{28,24},{5,1},{9,5},{13... | collective-permute-start | bytes 3145736 | tf_op jit(solution)/shard_map/ppermute | solution.py:17
  239.6 2.9 copy-start.30
  239.7 2.9 copy-start.19
  240.8 91.9 %collective-permute-start.3 = (f32[256,1024]{0,1:T(8,128)}, f32[256,1024]{0,1:T(8,128)}, u32[]{:S(2)}, u32[]{:S(2)}) collective-permute-start(f32[256,1024]{0,1:T(8,128)} %pad_add_fusion), channel_id=1, source_target_pairs={{4,0},{8,4},{12,8},{16,12},{20,16},{24,20},{28,24},{5,1},{9,5},{13... | collective-permute-start | bytes 3145736 | tf_op jit(solution)/shard_map/ppermute | solution.py:17
  244.9 83.1 %copy-start.4 = (f32[1,256,8,128]{1,3,2,0:T(8,128)S(1)}, f32[1,256,8,128]{1,3,2,0:T(8,128)}, u32[]{:S(2)}) copy-start(f32[1,256,8,128]{1,3,2,0:T(8,128)} %copy.166) | copy-start | bytes 3145732
  329.5 3.2 copy-start.6
  332.7 63.9 %copy-start.1 = (bf16[1,256,2048]{2,1,0:T(8,128)(2,1)S(1)}, bf16[1,256,2048]{2,1,0:T(8,128)(2,1)}, u32[]{:S(2)}) copy-start(bf16[1,256,2048]{2,1,0:T(8,128)(2,1)} %param.9) | copy-start | bytes 3145732
  (17 other events, 26.1 us)
Sparse Core Ops, SparseCore 0:
  10.7 58.8 all-gather.3
  71.7 48.3 all-gather.5
  121.6 32.9 all-gather.7
  157.1 71.3 reduce-scatter.2
  231.9 92.0 all-reduce.6
  328.0 68.5 reduce-scatter.4
